TPU v7x, 256 devices: a whole 4x4x8 slice. The times are simulated.
256 devices in a mesh: section: 4 (over x), seq: 64 (over y, z, core).
Axes of the slice: x: 4, y: 4, z: 8, core: 2. Of those that a mesh axis runs over, the one named last changes fastest.
Arguments:
- layer_input: bfloat16 [4, 4, 4096, 1536], P('section', None, 'seq'), may hold values from -16 to 16
- grad_top: bfloat16 [4, 4096, 1536], P(None, 'seq'), may hold values from -16 to 16
- w_conv: bfloat16 [4, 1536, 2304], P('section'), may hold values from -0.09375 to 0.09375
- w_out: bfloat16 [4, 1536, 768], P('section'), may hold values from -0.21875 to 0.21875
Outputs:
- grad_inputs: bfloat16 [4, 4, 4096, 1536], P('section', None, 'seq')
- w_conv_grad: float32 [4, 1536, 2304], P('section', 'seq')
- w_out_grad: float32 [4, 1536, 768], P('section', 'seq')
All inputs are finite; a program needn't handle non-finite values.
Results may differ from a plain program's by a relative error of at most 0.007.
Values may be sent and summed in bfloat16 or wider, within the bound.
A program may use at most 128 MiB of HBM per device.

v0:
```python
import functools
import math

import jax
import jax.numpy as jnp
from jax import lax
from jax.experimental import pallas as pl
from jax.experimental.pallas import tpu as pltpu
from jax.sharding import PartitionSpec as P

BF = jnp.bfloat16
F32 = jnp.float32
NY, NZ = 4, 8
RB = 48
HW = 384


def seq_place():
    j = lax.axis_index("seq")
    c = lax.rem(j, 2)
    z = lax.rem(lax.div(j, 2), NZ)
    y = lax.div(j, 2 * NZ)
    return y, z, c


def seq_at(y, z, c):
    return (y * NZ + z) * 2 + c


SEQS = 4
PB = 64
CH = 1536
FW = 768
DMAX = 64
NS = 4
NQ = 3
QW = CH // NQ


def ring_bufs(n, nb, wd):
    hn = n // 2
    wu = HW - wd
    out = []
    for _ in range(2):
        out += [
            pltpu.VMEM((nb, RB, wd), BF),
            pltpu.VMEM((nb, RB, wu), BF),
            pltpu.VMEM((hn - 1, nb, RB, HW), BF),
            pltpu.VMEM((hn - 1, nb, RB, HW), BF),
        ]
    return out


class Ring:
    def __init__(self, n, nb, wd, me, down, up, index, block, refs, sems, first):
        self.n, self.nb, self.wd, self.me = n, nb, wd, me
        self.down, self.up, self.index, self.block = down, up, index, block
        self.s0d, self.s0u, self.sd, self.su, self.r0d, self.r0u, self.rd, self.ru = refs
        self.send, self.recv = sems
        self.first = first
        self.copies = []
        self.last = None

    def copy(self, src, dst, to):
        k = self.first + len(self.copies)
        one = pltpu.make_async_remote_copy(
            src_ref=src, dst_ref=dst, send_sem=self.send.at[k], recv_sem=self.recv.at[k],
            device_id={"seq": to}, device_id_type=pl.DeviceIdType.MESH)
        one.start()
        self.copies.append(one)
        return one

    def each(self, body):
        if self.nb == 1:
            body(0)
        else:
            lax.fori_loop(0, self.nb, lambda k, t: (body(k), t)[1], 0)

    def start(self):
        dest = lax.rem(self.me + self.n // 2, self.n)
        wd = self.wd

        def body(k):
            own = self.block[self.index(k, dest)]
            self.s0d[k] = own[:, :wd].astype(BF)
            self.s0u[k] = own[:, wd:].astype(BF)

        self.each(body)
        self.last = (self.copy(self.s0d, self.r0d, self.down), self.copy(self.s0u, self.r0u, self.up))

    def step(self, i):
        away = self.n // 2 - i
        wd = self.wd
        dest_d = lax.rem(self.me + self.n - away, self.n)
        dest_u = lax.rem(self.me + away, self.n)
        prev_d, prev_u = self.last
        prev_d.wait_recv()

        def body_d(k):
            own = self.block[self.index(k, dest_d)]
            if i == 1:
                self.sd[i - 1, k, :, :wd] = (own[:, :wd] + self.r0d[k].astype(F32)).astype(BF)
                self.sd[i - 1, k, :, wd:] = own[:, wd:].astype(BF)
            else:
                self.sd[i - 1, k] = (own + self.rd[i - 2, k].astype(F32)).astype(BF)

        self.each(body_d)
        new_d = self.copy(self.sd.at[i - 1], self.rd.at[i - 1], self.down)
        prev_u.wait_recv()

        def body_u(k):
            own = self.block[self.index(k, dest_u)]
            if i == 1:
                self.su[i - 1, k, :, :wd] = own[:, :wd].astype(BF)
                self.su[i - 1, k, :, wd:] = (own[:, wd:] + self.r0u[k].astype(F32)).astype(BF)
            else:
                self.su[i - 1, k] = (own + self.ru[i - 2, k].astype(F32)).astype(BF)

        self.each(body_u)
        new_u = self.copy(self.su.at[i - 1], self.ru.at[i - 1], self.up)
        self.last = (new_d, new_u)

    def finish(self):
        end = self.n // 2 - 2
        for one in self.last:
            one.wait_recv()

        def body(k):
            at = self.index(k, self.me)
            self.block[at] = self.block[at] + (self.rd[end, k].astype(F32) + self.ru[end, k].astype(F32))

        self.each(body)

    def drain(self):
        for one in self.copies:
            one.wait_send()


ORDERS = ("zy", "zy", "yz", "yz")
SPLITS = (256, 128, 256, 128)


def rs_scratch():
    shapes = [pltpu.VMEM((NY, NZ, RB, HW), F32) for _ in range(4)]
    for order, wd in zip(ORDERS, SPLITS):
        if order == "zy":
            shapes += ring_bufs(NZ, NY, wd) + ring_bufs(NY, 1, wd)
        else:
            shapes += ring_bufs(NY, NZ, wd) + ring_bufs(NZ, 1, wd)
    shapes += [
        pltpu.VMEM((4, RB // 2, HW), F32),
        pltpu.VMEM((4, RB // 2, HW), F32),
        pltpu.SemaphoreType.DMA((49,)),
        pltpu.SemaphoreType.DMA((49,)),
    ]
    return shapes


def rs_run(fill, scale, conv_ref, out_ref, refs):
    y, z, c = seq_place()
    blocks = refs[:4]
    bufs = refs[4:4 + 64]
    xs, xr, send, recv = refs[68:72]
    zd, zu = seq_at(y, lax.rem(z + NZ - 1, NZ), c), seq_at(y, lax.rem(z + 1, NZ), c)
    yd, yu = seq_at(lax.rem(y + NY - 1, NY), z, c), seq_at(lax.rem(y + 1, NY), z, c)
    plans = []
    first = 0
    for b in range(4):
        block = blocks[b]
        one, two = bufs[16 * b:16 * b + 8], bufs[16 * b + 8:16 * b + 16]
        wd = SPLITS[b]
        if ORDERS[b] == "zy":
            r1 = Ring(NZ, NY, wd, z, zd, zu, lambda k, d: (k, d), block, one, (send, recv), first)
            r2 = Ring(NY, 1, wd, y, yd, yu, lambda k, d: (d, z), block, two, (send, recv), first + 8)
            plan = [functools.partial(r1.step, i) for i in (1, 2, 3)]
            plan += [lambda r1=r1, r2=r2: (r1.finish(), r2.start()), functools.partial(r2.step, 1), r2.finish]
        else:
            r1 = Ring(NY, NZ, wd, y, yd, yu, lambda k, d: (d, k), block, one, (send, recv), first)
            r2 = Ring(NZ, 1, wd, z, zd, zu, lambda k, d: (y, d), block, two, (send, recv), first + 4)
            plan = [functools.partial(r1.step, 1), lambda r1=r1, r2=r2: (r1.finish(), r2.start())]
            plan += [functools.partial(r2.step, i) for i in (1, 2, 3)] + [r2.finish]
        first += 12
        plans.append((r1, r2, plan))
    for b in (0, 2, 1, 3):
        fill(b, blocks[b])
        plans[b][0].start()
    for k in range(6):
        for b in (0, 2, 1, 3):
            plans[b][2][k]()
    half = RB // 2
    for b in range(4):
        xs[b] = blocks[b][y, z, pl.ds(pl.multiple_of((1 - c) * half, 8), half), :]
    swap = pltpu.make_async_remote_copy(
        src_ref=xs, dst_ref=xr, send_sem=send.at[48], recv_sem=recv.at[48],
        device_id={"seq": seq_at(y, z, 1 - c)}, device_id_type=pl.DeviceIdType.MESH)
    swap.start()

    def put(b, core, value):
        at = pl.multiple_of(core * HW, 128)
        if b == 3:
            out_ref[:, pl.ds(at, HW)] = value * scale
        else:
            conv_ref[:, pl.ds(pl.multiple_of(b * 2 * HW + at, 128), HW)] = value * scale

    for b in range(4):
        put(b, c, blocks[b][y, z, pl.ds(pl.multiple_of(c * half, 8), half), :])
    swap.wait_recv()
    for b in range(4):
        put(b, 1 - c, xr[b])
    swap.wait_send()
    for r1, r2, _ in plans:
        r1.drain()
        r2.drain()


def remote(src, dst, send, recv, to):
    return pltpu.make_async_remote_copy(
        src_ref=src, dst_ref=dst, send_sem=send, recv_sem=recv,
        device_id=to, device_id_type=pl.DeviceIdType.MESH)


def gelu_parts(v):
    cdf = 0.5 * (1.0 + lax.erf(v * 0.7071067811865476))
    return v * cdf, cdf + v * jnp.exp(-0.5 * v * v) * 0.3989422804014327


def loop(n, body):
    lax.fori_loop(0, n, lambda i, t: (body(i), t)[1], 0)


NAMES = (
    ("xv", (SEQS, PB, CH), BF), ("wc", (CH, 3 * FW), BF), ("wo", (CH, FW), BF),
    ("hx", (SEQS, 2, PB, CH), BF), ("ho", (SEQS, PB, CH), BF), ("gx", (SEQS, PB, CH), F32),
    ("exth", (3 * PB, CH), F32), ("uf", (PB, FW), F32), ("su", (SEQS, PB, FW), F32),
    ("gf", (SEQS, PB, FW), BF), ("gg", (SEQS, 2, PB, HW), BF),
    ("ct", (SEQS, 2, PB, CH), BF), ("dux", (SEQS, PB, FW), BF), ("dup", (SEQS, PB, FW), BF),
    ("duo", (SEQS, PB, FW), BF), ("extd", (3 * PB, FW), F32), ("dwin", (SEQS, PB, 3 * FW), BF),
    ("dw", (SEQS, 2, PB, 3 * HW), BF), ("dnx", (SEQS, PB, CH), BF),
    ("hT", (NY, HW, 2 * SEQS * PB), BF), ("cT", (NY, HW, 2 * SEQS * PB), BF),
)
SEMS = (
    ("s_x", (SEQS,)), ("s_w", (2,)), ("s_top", (SEQS,)), ("s_out", (SEQS,)),
    ("hp_s", (SEQS,)), ("hp_r", (SEQS,)), ("ho_s", (SEQS,)), ("ho_r", (SEQS,)),
    ("g_s", (SEQS,)), ("g_r", (SEQS,)), ("c_s", (SEQS, NQ)), ("c_r", (SEQS, NQ)),
    ("dp_s", (SEQS,)), ("dp_r", (SEQS,)), ("do_s", (SEQS,)), ("do_r", (SEQS,)),
    ("dw_s", (SEQS, 3)), ("dw_r", (SEQS, 3)), ("hop_s", (SEQS, NQ)), ("hop_r", (SEQS, NQ)),
)


def step_kernel(scale, x_hbm, top_hbm, wc_hbm, wo_hbm, din_hbm, conv_ref, out_ref, *refs):
    r = dict(zip([n[0] for n in NAMES] + [n[0] for n in SEMS], refs))
    ring_refs = refs[len(NAMES) + len(SEMS):]
    xv, wc, wo, hx, ho, gx, exth, uf, su = (r[k] for k in ("xv", "wc", "wo", "hx", "ho", "gx", "exth", "uf", "su"))
    gf, gg, ct, dux, dup, duo, extd = (r[k] for k in ("gf", "gg", "ct", "dux", "dup", "duo", "extd"))
    dwin, dw, dnx, hT, cT = (r[k] for k in ("dwin", "dw", "dnx", "hT", "cT"))
    y, z, c = seq_place()
    s = lax.axis_index("section")
    j = seq_at(y, z, c)
    d = lax.shift_left(jnp.int32(DMAX // 2 ** (NS - 1)), s)
    partner = {"seq": seq_at(y, z, 1 - c)}
    outer_at = lax.rem(j + 2 * NY * NZ + 2 * c - 1, 2 * NY * NZ)
    outer = {"seq": outer_at}
    edge = jnp.logical_or(jnp.logical_and(c == 0, j == 0), jnp.logical_and(c == 1, j == 2 * NY * NZ - 1))
    barrier = pltpu.get_barrier_semaphore()
    for to in (partner, outer,
               {"seq": seq_at(y, lax.rem(z + NZ - 1, NZ), c)}, {"seq": seq_at(y, lax.rem(z + 1, NZ), c)},
               {"seq": seq_at(lax.rem(y + NY - 1, NY), z, c)}, {"seq": seq_at(lax.rem(y + 1, NY), z, c)},
               {"section": lax.rem(s + NS - 1, NS)}, {"section": lax.rem(s + 1, NS)}):
        pl.semaphore_signal(barrier, inc=1, device_id=to, device_id_type=pl.DeviceIdType.MESH)

    def mine(t):
        return pl.ds(pl.multiple_of(t * FW + c * HW, 128), HW)

    def theirs(t):
        return pl.ds(pl.multiple_of(t * FW + (1 - c) * HW, 128), HW)

    def part(q):
        return slice(q * QW, (q + 1) * QW)

    load_x = lambda b: pltpu.make_async_copy(x_hbm.at[0, b], xv.at[b], r["s_x"].at[b])
    load_wc = pltpu.make_async_copy(wc_hbm.at[0], wc, r["s_w"].at[0])
    load_wo = pltpu.make_async_copy(wo_hbm.at[0], wo, r["s_w"].at[1])
    load_top = lambda b: pltpu.make_async_copy(top_hbm.at[b], ct.at[b, 0], r["s_top"].at[b])
    save = lambda b: pltpu.make_async_copy(dnx.at[b], din_hbm.at[0, b], r["s_out"].at[b])
    h_near = lambda b: remote(hx.at[b, 0], hx.at[b, 1], r["hp_s"].at[b], r["hp_r"].at[b], partner)
    h_far = lambda b: remote(hx.at[b, 0], ho.at[b], r["ho_s"].at[b], r["ho_r"].at[b], outer)
    g_near = lambda b: remote(gf.at[b, :, theirs(0)], gg.at[b, 1], r["g_s"].at[b], r["g_r"].at[b], partner)
    c_near = lambda b, q: remote(ct.at[b, 0, :, part(q)], ct.at[b, 1, :, part(q)], r["c_s"].at[b, q], r["c_r"].at[b, q], partner)
    d_near = lambda b: remote(dux.at[b], dup.at[b], r["dp_s"].at[b], r["dp_r"].at[b], partner)
    d_far = lambda b: remote(dux.at[b], duo.at[b], r["do_s"].at[b], r["do_r"].at[b], outer)
    w_near = lambda b, t: remote(dwin.at[b, :, theirs(t)], dw.at[b, 1, :, pl.ds(t * HW, HW)], r["dw_s"].at[b, t], r["dw_r"].at[b, t], partner)
    hop = lambda b, q: remote(dnx.at[b, :, part(q)], ct.at[b, 0, :, part(q)], r["hop_s"].at[b, q], r["hop_r"].at[b, q],
                              {"section": lax.max(s - 1, 0)})

    for b in range(SEQS):
        load_x(b).start()
    load_wc.start()

    @pl.when(s == NS - 1)
    def _():
        for b in range(SEQS):
            load_top(b).start()

    load_wo.start()

    def forward_in(b):
        load_x(b).wait()

        def rows(i):
            at = pl.ds(pl.multiple_of(i * 16, 16), 16)
            for n in range(2):
                cols = slice(n * FW, (n + 1) * FW)
                h, slope = gelu_parts(xv[b, at, cols].astype(F32))
                hx[b, 0, at, cols] = h.astype(BF)
                gx[b, at, cols] = slope

        loop(PB // 16, rows)

        @pl.when(b == 0)
        def _():
            pl.semaphore_wait(barrier, 8)

        h_far(b).start()
        h_near(b).start()

    loop(SEQS, forward_in)
    load_wc.wait()
    load_wo.wait()
    own_at = pl.ds(PB, PB)
    near_at = pl.ds(pl.multiple_of((1 - c) * 2 * PB, PB), PB)
    far_at = pl.ds(pl.multiple_of(c * 2 * PB, PB), PB)

    def forward_mid(b):
        h_near(b).wait_recv()
        h_far(b).wait_recv()
        exth[own_at] = hx[b, 0].astype(F32)
        exth[near_at] = hx[b, 1].astype(F32)
        exth[far_at] = jnp.where(edge, 0.0, ho[b].astype(F32))
        acc = None
        for t in range(3):
            at = pl.ds(pl.multiple_of(PB + (t - 1) * d, 8), PB)
            got = jnp.dot(exth[at].astype(BF), wc[:, t * FW:(t + 1) * FW], preferred_element_type=F32)
            acc = got if acc is None else acc + got
        uf[...] = acc

        def rows(i):
            at = pl.ds(pl.multiple_of(i * 16, 16), 16)
            g, slope = gelu_parts(uf[at])
            gf[b, at] = g.astype(BF)
            su[b, at] = slope

        loop(PB // 16, rows)
        gg[b, 0] = gf[b, :, mine(0)]
        g_near(b).start()

    def turn(src, dst, b):
        at = pl.ds(pl.multiple_of(b * 2 * PB, 2 * PB), 2 * PB)
        for m in range(NY):
            dst[m, :, at] = src[b, :, :, m * HW:(m + 1) * HW].reshape(2 * PB, HW).T

    @pl.when(s < NS - 1)
    def _():
        loop(SEQS, forward_mid)
        loop(SEQS, lambda b: turn(hx, hT, b))

    def backward(b):
        @pl.when(s == NS - 1)
        def _():
            forward_mid(b)
            load_top(b).wait()

        dg = None
        for q in range(NQ):
            @pl.when(s < NS - 1)
            def _():
                hop(b, q).wait_recv()

            c_near(b, q).start()
            got = jnp.dot(ct[b, 0, :, part(q)], wo[q * QW:(q + 1) * QW], preferred_element_type=F32)
            dg = got if dg is None else dg + got
        du = (dg * su[b]).astype(BF)
        dux[b] = du
        d_far(b).start()
        d_near(b).start()
        extd[own_at] = du.astype(F32)
        d_near(b).wait_recv()
        extd[near_at] = dup[b].astype(F32)
        d_far(b).wait_recv()
        extd[far_at] = jnp.where(edge, 0.0, duo[b].astype(F32))
        for t in range(3):
            at = pl.ds(pl.multiple_of(PB - (t - 1) * d, 8), PB)
            dwin[b, :, t * FW:(t + 1) * FW] = extd[at].astype(BF)
        for q in range(NQ):
            dh = lax.dot_general(dwin[b], wc[q * QW:(q + 1) * QW], (((1,), (1,)), ((), ())), preferred_element_type=F32)
            dnx[b, :, part(q)] = (ct[b, 0, :, part(q)].astype(F32) + dh * gx[b, :, part(q)]).astype(BF)

            @pl.when(s > 0)
            def _():
                hop(b, q).start()

        save(b).start()
        for t in range(3):
            w_near(b, t).start()
            dw[b, 0, :, t * HW:(t + 1) * HW] = dwin[b, :, mine(t)]
        for q in range(NQ):
            c_near(b, q).wait_recv()
        turn(ct, cT, b)

    loop(SEQS, backward)

    @pl.when(s == NS - 1)
    def _():
        loop(SEQS, lambda b: turn(hx, hT, b))

    def gathered(b):
        for t in range(3):
            w_near(b, t).wait_recv()
        g_near(b).wait_recv()

    loop(SEQS, gathered)

    def fill(b, block):
        lhs = cT if b == 3 else hT
        for m in range(NY):
            rhs = gg[...] if b == 3 else dw[:, :, :, b * HW:(b + 1) * HW]
            got = jnp.dot(lhs[m], rhs.reshape(2 * SEQS * PB, HW), preferred_element_type=F32)
            block[m] = got.reshape(NZ, RB, HW)

    rs_run(fill, scale, conv_ref, out_ref, ring_refs)

    def ended(b):
        save(b).wait()
        h_near(b).wait_send()
        h_far(b).wait_send()
        g_near(b).wait_send()
        d_near(b).wait_send()
        d_far(b).wait_send()
        for t in range(3):
            w_near(b, t).wait_send()
        for q in range(NQ):
            c_near(b, q).wait_send()

            @pl.when(s > 0)
            def _():
                hop(b, q).wait_send()

    loop(SEQS, ended)


def body(layer_input, grad_top, w_conv, w_out):
    scale = 1.0 / math.sqrt(SEQS * PB * 2 * NY * NZ)
    scratch = [pltpu.VMEM(shape, kind) for _, shape, kind in NAMES]
    scratch += [pltpu.SemaphoreType.DMA(shape) for _, shape in SEMS]
    scratch += rs_scratch()
    dinput, conv_grad, out_grad = pl.pallas_call(
        functools.partial(step_kernel, scale),
        out_shape=(
            jax.ShapeDtypeStruct((1, SEQS, PB, CH), BF),
            jax.ShapeDtypeStruct((CH // (2 * NY * NZ), 3 * FW), F32),
            jax.ShapeDtypeStruct((CH // (2 * NY * NZ), FW), F32),
        ),
        in_specs=[pl.BlockSpec(memory_space=pl.ANY)] * 4,
        out_specs=(
            pl.BlockSpec(memory_space=pl.ANY),
            pl.BlockSpec(memory_space=pltpu.VMEM),
            pl.BlockSpec(memory_space=pltpu.VMEM),
        ),
        scratch_shapes=scratch,
        compiler_params=pltpu.CompilerParams(collective_id=1, has_side_effects=True, vmem_limit_bytes=63 << 20),
    )(layer_input, grad_top, w_conv, w_out)
    return (dinput, conv_grad[None], out_grad[None])


def solution(mesh):
    return jax.shard_map(
        body,
        mesh=mesh,
        in_specs=(
            P("section", None, "seq", None),
            P(None, "seq", None),
            P("section", None, None),
            P("section", None, None),
        ),
        out_specs=(
            P("section", None, "seq", None),
            P("section", "seq", None),
            P("section", "seq", None),
        ),
        check_vma=False,
    )
```

profile of v0, /device:TPU:1, one launch (start us, length us, event | category | flops | bytes accessed | tf_op | source)
XLA Modules:
  0.0 137.9 jit_solution(13440867752931607013)
XLA Ops:
  0.6 132.0 %shard_map.67 = (bf16[1,4,64,1536]{3,2,1,0:T(8,128)(2,1)}, f32[24,2304]{1,0:T(8,128)}, f32[24,768]{1,0:T(8,128)}) custom-call(bf16[1,4,64,1536]{3,2,1,0:T(8,128)(2,1)} %x_hbm.1, bf16[4,64,1536]{2,1,0:T(8,128)(2,1)} %top_hbm.1, bf16[1,1536,2304]{2,1,0:T(8,128)(2,1)} %wc_hbm.1, bf16[1,1536,768]{2,1,0:T(8,128)(2,1)} %wo_hbm.1), custom_call_target="tpu_custom_call" | custom-call | tf_op jit(solution)/shard_map/pallas_call | solution.py:455
  132.7 2.1 %copy.10 = bf16[1,4,64,1536]{3,2,1,0:T(8,128)(2,1)} copy(bf16[1,4,64,1536]{3,2,1,0:T(8,128)(2,1)} %get-tuple-element.12) | data formatting | bytes 1572864
  134.7 1.6 %copy.11 = f32[1,24,2304]{2,1,0:T(8,128)} copy(f32[1,24,2304]{2,1,0:T(8,128)} %bitcast.2) | data formatting | bytes 442368
  136.4 1.5 %copy.12 = f32[1,24,768]{2,1,0:T(8,128)} copy(f32[1,24,768]{2,1,0:T(8,128)} %bitcast.3) | data formatting | bytes 147456
where the time goes:
time: 138 us
  Pallas kernels  132 us (96%)
  local copies, waits for them, and re-layouts  5.22 us (4%)
    pallas_call x1, Pallas kernels, body(): pl.pallas_call(functools.partial(step_kernel, scale), out_shape=(jax.Shap...  132 us
    unnamed x3, local copies, waits for them, and re-layouts  5.22 us

commit v1 on v0

--- a/solution.py
+++ b/solution.py
@@ -138,6 +138,10 @@
 
 ORDERS = ("zy", "zy", "yz", "yz")
 SPLITS = (256, 128, 256, 128)
+ISSUE = (
+    (2, 0), (0, 0), (1, 0), (3, 0), (0, 1), (2, 1), (1, 1), (3, 1), (0, 2), (1, 2), (2, 2), (0, 3), (1, 3), (2, 3),
+    (3, 2), (0, 4), (0, 5), (1, 4), (2, 4), (3, 3), (0, 6), (1, 5), (2, 5), (3, 4), (1, 6), (2, 6), (3, 5), (3, 6),
+)
 
 
 def rs_scratch():
@@ -181,12 +185,12 @@
             plan += [functools.partial(r2.step, i) for i in (1, 2, 3)] + [r2.finish]
         first += 12
         plans.append((r1, r2, plan))
-    for b in (0, 2, 1, 3):
-        fill(b, blocks[b])
-        plans[b][0].start()
-    for k in range(6):
-        for b in (0, 2, 1, 3):
-            plans[b][2][k]()
+    for b, k in ISSUE:
+        if k == 0:
+            fill(b, blocks[b])
+            plans[b][0].start()
+        else:
+            plans[b][2][k - 1]()
     half = RB // 2
     for b in range(4):
         xs[b] = blocks[b][y, z, pl.ds(pl.multiple_of((1 - c) * half, 8), half), :]
@@ -229,7 +233,7 @@
 
 
 NAMES = (
-    ("xv", (SEQS, PB, CH), BF), ("wc", (CH, 3 * FW), BF), ("wo", (CH, FW), BF),
+    ("xv", (SEQS, PB, CH), BF), ("wc", (CH, 3 * FW), BF), ("wt", (3 * FW, CH), BF), ("wo", (CH, FW), BF),
     ("hx", (SEQS, 2, PB, CH), BF), ("ho", (SEQS, PB, CH), BF), ("gx", (SEQS, PB, CH), F32),
     ("exth", (3 * PB, CH), F32), ("uf", (PB, FW), F32), ("su", (SEQS, PB, FW), F32),
     ("gf", (SEQS, PB, FW), BF), ("gg", (SEQS, 2, PB, HW), BF),
@@ -250,6 +254,7 @@
 def step_kernel(scale, x_hbm, top_hbm, wc_hbm, wo_hbm, din_hbm, conv_ref, out_ref, *refs):
     r = dict(zip([n[0] for n in NAMES] + [n[0] for n in SEMS], refs))
     ring_refs = refs[len(NAMES) + len(SEMS):]
+    wt = r["wt"]
     xv, wc, wo, hx, ho, gx, exth, uf, su = (r[k] for k in ("xv", "wc", "wo", "hx", "ho", "gx", "exth", "uf", "su"))
     gf, gg, ct, dux, dup, duo, extd = (r[k] for k in ("gf", "gg", "ct", "dux", "dup", "duo", "extd"))
     dwin, dw, dnx, hT, cT = (r[k] for k in ("dwin", "dw", "dnx", "hT", "cT"))
@@ -287,7 +292,15 @@
     g_near = lambda b: remote(gf.at[b, :, theirs(0)], gg.at[b, 1], r["g_s"].at[b], r["g_r"].at[b], partner)
     c_near = lambda b, q: remote(ct.at[b, 0, :, part(q)], ct.at[b, 1, :, part(q)], r["c_s"].at[b, q], r["c_r"].at[b, q], partner)
     d_near = lambda b: remote(dux.at[b], dup.at[b], r["dp_s"].at[b], r["dp_r"].at[b], partner)
-    d_far = lambda b: remote(dux.at[b], duo.at[b], r["do_s"].at[b], r["do_r"].at[b], outer)
+
+    def d_far(b, act):
+        for n, here in ((16, s < NS - 2), (32, s == NS - 2), (64, s == NS - 1)):
+            at = pl.ds(pl.multiple_of(c * (PB - n), 16), n)
+
+            @pl.when(here)
+            def _():
+                act(remote(dux.at[b, at], duo.at[b, at], r["do_s"].at[b], r["do_r"].at[b], outer))
+
     w_near = lambda b, t: remote(dwin.at[b, :, theirs(t)], dw.at[b, 1, :, pl.ds(t * HW, HW)], r["dw_s"].at[b, t], r["dw_r"].at[b, t], partner)
     hop = lambda b, q: remote(dnx.at[b, :, part(q)], ct.at[b, 0, :, part(q)], r["hop_s"].at[b, q], r["hop_r"].at[b, q],
                               {"section": lax.max(s - 1, 0)})
@@ -320,11 +333,21 @@
         def _():
             pl.semaphore_wait(barrier, 8)
 
-        h_far(b).start()
+        @pl.when(jnp.logical_or(s < NS - 1, b < 2))
+        def _():
+            h_far(b).start()
+
         h_near(b).start()
 
     loop(SEQS, forward_in)
     load_wc.wait()
+
+    def flip(n):
+        at = pl.ds(pl.multiple_of(n * 256, 256), 256)
+        for m in range(CH // 256):
+            wt[at, m * 256:(m + 1) * 256] = wc[m * 256:(m + 1) * 256, at].T
+
+    loop(3 * FW // 256, flip)
     load_wo.wait()
     own_at = pl.ds(PB, PB)
     near_at = pl.ds(pl.multiple_of((1 - c) * 2 * PB, PB), PB)
@@ -363,35 +386,53 @@
         loop(SEQS, forward_mid)
         loop(SEQS, lambda b: turn(hx, hT, b))
 
-    def backward(b):
-        @pl.when(s == NS - 1)
-        def _():
-            forward_mid(b)
-            load_top(b).wait()
-
+    def front(b):
         dg = None
         for q in range(NQ):
             @pl.when(s < NS - 1)
             def _():
                 hop(b, q).wait_recv()
 
-            c_near(b, q).start()
             got = jnp.dot(ct[b, 0, :, part(q)], wo[q * QW:(q + 1) * QW], preferred_element_type=F32)
             dg = got if dg is None else dg + got
-        du = (dg * su[b]).astype(BF)
-        dux[b] = du
-        d_far(b).start()
+        dux[b] = (dg * su[b]).astype(BF)
+        d_far(b, lambda one: one.start())
         d_near(b).start()
-        extd[own_at] = du.astype(F32)
+        for q in range(NQ):
+            c_near(b, q).start()
+
+    def first_front(b):
+        forward_mid(b)
+        load_top(b).wait()
+        front(b)
+
+        @pl.when(b < SEQS - 2)
+        def _():
+            h_far(b + 2).start()
+
+    @pl.when(s == NS - 1)
+    def _():
+        first_front(0)
+
+    def backward(b):
+        @pl.when(s < NS - 1)
+        def _():
+            front(b)
+
+        @pl.when(jnp.logical_and(s == NS - 1, b < SEQS - 1))
+        def _():
+            first_front(b + 1)
+
+        extd[own_at] = dux[b].astype(F32)
         d_near(b).wait_recv()
         extd[near_at] = dup[b].astype(F32)
-        d_far(b).wait_recv()
+        d_far(b, lambda one: one.wait_recv())
         extd[far_at] = jnp.where(edge, 0.0, duo[b].astype(F32))
         for t in range(3):
             at = pl.ds(pl.multiple_of(PB - (t - 1) * d, 8), PB)
             dwin[b, :, t * FW:(t + 1) * FW] = extd[at].astype(BF)
         for q in range(NQ):
-            dh = lax.dot_general(dwin[b], wc[q * QW:(q + 1) * QW], (((1,), (1,)), ((), ())), preferred_element_type=F32)
+            dh = jnp.dot(dwin[b], wt[:, part(q)], preferred_element_type=F32)
             dnx[b, :, part(q)] = (ct[b, 0, :, part(q)].astype(F32) + dh * gx[b, :, part(q)]).astype(BF)
 
             @pl.when(s > 0)
@@ -434,7 +475,7 @@
         h_far(b).wait_send()
         g_near(b).wait_send()
         d_near(b).wait_send()
-        d_far(b).wait_send()
+        d_far(b, lambda one: one.wait_send())
         for t in range(3):
             w_near(b, t).wait_send()
         for q in range(NQ):
@@ -445,6 +486,12 @@
                 hop(b, q).wait_send()
 
     loop(SEQS, ended)
+
+
+def pass_on(a, b, c, a_out, b_out, c_out):
+    a_out[...] = a[...]
+    b_out[...] = b[...]
+    c_out[...] = c[...]
 
 
 def body(layer_input, grad_top, w_conv, w_out):
@@ -468,7 +515,13 @@
         scratch_shapes=scratch,
         compiler_params=pltpu.CompilerParams(collective_id=1, has_side_effects=True, vmem_limit_bytes=63 << 20),
     )(layer_input, grad_top, w_conv, w_out)
-    return (dinput, conv_grad[None], out_grad[None])
+    results = (dinput, conv_grad[None], out_grad[None])
+    return pl.pallas_call(
+        pass_on,
+        out_shape=tuple(jax.ShapeDtypeStruct(one.shape, one.dtype) for one in results),
+        in_specs=[pl.BlockSpec(memory_space=pltpu.VMEM)] * 3,
+        out_specs=(pl.BlockSpec(memory_space=pltpu.VMEM),) * 3,
+    )(*results)
 
 
 def solution(mesh):

time: 138 us -> 123 us (0.89)
  Pallas kernels: 132 us -> 122 us
  local copies, waits for them, and re-layouts: 5.22 us -> 0 us
    pallas_call x1, Pallas kernels: 132 us -> 120 us  [body(): pl.pallas_call(functools.partial(step_kernel, scale), out_shape=(jax.Shap...]
    unnamed x3 -> x0, local copies, waits for them, and re-layouts: 5.22 us -> none
    pallas_call x0 -> x1, Pallas kernels: none -> 2.24 us  [body(): pl.pallas_call(pass_on, out_shape=tuple((jax.ShapeDtypeStruct(one.shape,...]
where the time goes in v1:
time: 123 us
  Pallas kernels  122 us (99%)
    pallas_call x1, Pallas kernels, body(): pl.pallas_call(functools.partial(step_kernel, scale), out_shape=(jax.Shap...  120 us

profile of v1, /device:TPU:1, one launch (start us, length us, event | category | flops | bytes accessed | tf_op | source)
XLA Modules:
  0.0 122.9 jit_solution(9224344279684193556)
XLA Ops:
  0.6 120.0 %shard_map.67 = (bf16[1,4,64,1536]{3,2,1,0:T(8,128)(2,1)}, f32[24,2304]{1,0:T(8,128)}, f32[24,768]{1,0:T(8,128)}) custom-call(bf16[1,4,64,1536]{3,2,1,0:T(8,128)(2,1)} %x_hbm.1, bf16[4,64,1536]{2,1,0:T(8,128)(2,1)} %top_hbm.1, bf16[1,1536,2304]{2,1,0:T(8,128)(2,1)} %wc_hbm.1, bf16[1,1536,768]{2,1,0:T(8,128)(2,1)} %wo_hbm.1), custom_call_target="tpu_custom_call" | custom-call | tf_op jit(solution)/shard_map/pallas_call | solution.py:502
  120.7 2.2 %shard_map.68 = (bf16[1,4,64,1536]{3,2,1,0:T(8,128)(2,1)}, f32[1,24,2304]{2,1,0:T(8,128)}, f32[1,24,768]{2,1,0:T(8,128)}) custom-call(bf16[1,4,64,1536]{3,2,1,0:T(8,128)(2,1)} %get-tuple-element.6.a, f32[1,24,2304]{2,1,0:T(8,128)} %bitcast.2, f32[1,24,768]{2,1,0:T(8,128)} %bitcast.3), custom_call_target="tpu_custom_call" | custom-call | tf_op jit(solution)/shard_map/pallas_call | solution.py:519

commit v2 on v1

--- a/solution.py
+++ b/solution.py
@@ -61,14 +61,16 @@
         self.copies = []
         self.last = None
 
-    def copy(self, src, dst, to):
+    def copy(self, ends, to):
         k = self.first + len(self.copies)
-        one = pltpu.make_async_remote_copy(
-            src_ref=src, dst_ref=dst, send_sem=self.send.at[k], recv_sem=self.recv.at[k],
-            device_id={"seq": to}, device_id_type=pl.DeviceIdType.MESH)
-        one.start()
-        self.copies.append(one)
-        return one
+
+        def make():
+            src, dst = ends()
+            return remote(src, dst, self.send.at[k], self.recv.at[k], {"seq": to})
+
+        make().start()
+        self.copies.append(make)
+        return make
 
     def each(self, body):
         if self.nb == 1:
@@ -86,7 +88,7 @@
             self.s0u[k] = own[:, wd:].astype(BF)
 
         self.each(body)
-        self.last = (self.copy(self.s0d, self.r0d, self.down), self.copy(self.s0u, self.r0u, self.up))
+        self.last = (self.copy(lambda: (self.s0d, self.r0d), self.down), self.copy(lambda: (self.s0u, self.r0u), self.up))
 
     def step(self, i):
         away = self.n // 2 - i
@@ -94,7 +96,7 @@
         dest_d = lax.rem(self.me + self.n - away, self.n)
         dest_u = lax.rem(self.me + away, self.n)
         prev_d, prev_u = self.last
-        prev_d.wait_recv()
+        prev_d().wait_recv()
 
         def body_d(k):
             own = self.block[self.index(k, dest_d)]
@@ -105,8 +107,8 @@
                 self.sd[i - 1, k] = (own + self.rd[i - 2, k].astype(F32)).astype(BF)
 
         self.each(body_d)
-        new_d = self.copy(self.sd.at[i - 1], self.rd.at[i - 1], self.down)
-        prev_u.wait_recv()
+        new_d = self.copy(lambda: (self.sd.at[i - 1], self.rd.at[i - 1]), self.down)
+        prev_u().wait_recv()
 
         def body_u(k):
             own = self.block[self.index(k, dest_u)]
@@ -117,13 +119,13 @@
                 self.su[i - 1, k] = (own + self.ru[i - 2, k].astype(F32)).astype(BF)
 
         self.each(body_u)
-        new_u = self.copy(self.su.at[i - 1], self.ru.at[i - 1], self.up)
+        new_u = self.copy(lambda: (self.su.at[i - 1], self.ru.at[i - 1]), self.up)
         self.last = (new_d, new_u)
 
     def finish(self):
         end = self.n // 2 - 2
         for one in self.last:
-            one.wait_recv()
+            one().wait_recv()
 
         def body(k):
             at = self.index(k, self.me)
@@ -133,43 +135,56 @@
 
     def drain(self):
         for one in self.copies:
-            one.wait_send()
-
-
-ORDERS = ("zy", "zy", "yz", "yz")
-SPLITS = (256, 128, 256, 128)
+            one().wait_send()
+
+
+ORDERS = ("zy", "yz", "yz", "zy", "yz")
+SPLITS = (256, 256, 128, 128, 256)
+NB = 5
 ISSUE = (
-    (2, 0), (0, 0), (1, 0), (3, 0), (0, 1), (2, 1), (1, 1), (3, 1), (0, 2), (1, 2), (2, 2), (0, 3), (1, 3), (2, 3),
-    (3, 2), (0, 4), (0, 5), (1, 4), (2, 4), (3, 3), (0, 6), (1, 5), (2, 5), (3, 4), (1, 6), (2, 6), (3, 5), (3, 6),
+    (1, 0), (0, 0), (3, 0), (2, 0), (4, 0), (0, 1), (1, 1), (3, 1), (2, 1), (4, 1), (0, 2), (3, 2),
+    (1, 2), (0, 3), (3, 3), (1, 3), (2, 2), (4, 2), (0, 4), (0, 5), (3, 4), (1, 4), (2, 3), (4, 3),
+    (0, 6), (3, 5), (1, 5), (2, 4), (4, 4), (3, 6), (1, 6), (2, 5), (4, 5), (2, 6), (4, 6),
 )
 
 
 def rs_scratch():
-    shapes = [pltpu.VMEM((NY, NZ, RB, HW), F32) for _ in range(4)]
+    shapes = [pltpu.VMEM((NY, NZ, RB, HW), F32) for _ in range(NB)]
     for order, wd in zip(ORDERS, SPLITS):
         if order == "zy":
             shapes += ring_bufs(NZ, NY, wd) + ring_bufs(NY, 1, wd)
         else:
             shapes += ring_bufs(NY, NZ, wd) + ring_bufs(NZ, 1, wd)
     shapes += [
-        pltpu.VMEM((4, RB // 2, HW), F32),
-        pltpu.VMEM((4, RB // 2, HW), F32),
-        pltpu.SemaphoreType.DMA((49,)),
-        pltpu.SemaphoreType.DMA((49,)),
+        pltpu.VMEM((NB, RB // 2, HW), F32),
+        pltpu.VMEM((NB, RB // 2, HW), F32),
+        pltpu.VMEM((RB // 2, 2 * HW), F32),
+        pltpu.VMEM((RB // 2, 2 * HW), F32),
+        pltpu.SemaphoreType.DMA((12 * NB + 4,)),
+        pltpu.SemaphoreType.DMA((12 * NB + 4,)),
     ]
     return shapes
 
 
-def rs_run(fill, scale, conv_ref, out_ref, refs):
+def rs_run(fill, beside, scale, conv_ref, out_ref, refs):
     y, z, c = seq_place()
-    blocks = refs[:4]
-    bufs = refs[4:4 + 64]
-    xs, xr, send, recv = refs[68:72]
+    s = lax.axis_index("section")
+    conds = (None, None, None, s > 0, s == NS - 1)
+
+    def guarded(b, act):
+        if conds[b] is None:
+            act()
+        else:
+            pl.when(conds[b])(lambda: (act(), None)[1])
+
+    blocks = refs[:NB]
+    bufs = refs[NB:NB + 16 * NB]
+    xs, xr, total, below, send, recv = refs[17 * NB:17 * NB + 6]
     zd, zu = seq_at(y, lax.rem(z + NZ - 1, NZ), c), seq_at(y, lax.rem(z + 1, NZ), c)
     yd, yu = seq_at(lax.rem(y + NY - 1, NY), z, c), seq_at(lax.rem(y + 1, NY), z, c)
     plans = []
     first = 0
-    for b in range(4):
+    for b in range(NB):
         block = blocks[b]
         one, two = bufs[16 * b:16 * b + 8], bufs[16 * b + 8:16 * b + 16]
         wd = SPLITS[b]
@@ -185,36 +200,69 @@
             plan += [functools.partial(r2.step, i) for i in (1, 2, 3)] + [r2.finish]
         first += 12
         plans.append((r1, r2, plan))
-    for b, k in ISSUE:
+    for n, (b, k) in enumerate(ISSUE):
+        if n == NB:
+            beside()
         if k == 0:
-            fill(b, blocks[b])
-            plans[b][0].start()
+            guarded(b, lambda b=b: (fill(b, blocks[b]), plans[b][0].start()))
         else:
-            plans[b][2][k - 1]()
+            guarded(b, plans[b][2][k - 1])
     half = RB // 2
-    for b in range(4):
-        xs[b] = blocks[b][y, z, pl.ds(pl.multiple_of((1 - c) * half, 8), half), :]
-    swap = pltpu.make_async_remote_copy(
-        src_ref=xs, dst_ref=xr, send_sem=send.at[48], recv_sem=recv.at[48],
-        device_id={"seq": seq_at(y, z, 1 - c)}, device_id_type=pl.DeviceIdType.MESH)
-    swap.start()
-
-    def put(b, core, value):
-        at = pl.multiple_of(core * HW, 128)
-        if b == 3:
-            out_ref[:, pl.ds(at, HW)] = value * scale
-        else:
-            conv_ref[:, pl.ds(pl.multiple_of(b * 2 * HW + at, 128), HW)] = value * scale
-
-    for b in range(4):
-        put(b, c, blocks[b][y, z, pl.ds(pl.multiple_of(c * half, 8), half), :])
-    swap.wait_recv()
-    for b in range(4):
-        put(b, 1 - c, xr[b])
-    swap.wait_send()
-    for r1, r2, _ in plans:
-        r1.drain()
-        r2.drain()
+    partner = {"seq": seq_at(y, z, 1 - c)}
+    conv_swap, low_swap, own_swap = (
+        remote(xs.at[at], xr.at[at], send.at[12 * NB + n], recv.at[12 * NB + n], partner)
+        for n, at in enumerate((pl.ds(0, 3), pl.ds(3, 1), pl.ds(4, 1))))
+    lower = remote(total, below, send.at[12 * NB + 3], recv.at[12 * NB + 3], {"section": lax.max(s - 1, 0)})
+
+    def rows(b, core):
+        return blocks[b][y, z, pl.ds(pl.multiple_of(core * half, 8), half), :]
+
+    def put(ref, at, core, value):
+        ref[:, pl.ds(pl.multiple_of(at + core * HW, 128), HW)] = value * scale
+
+    def swap(one, first, count):
+        for b in range(first, first + count):
+            xs[b] = rows(b, 1 - c)
+        one.start()
+
+    swap(conv_swap, 0, 3)
+    guarded(3, lambda: swap(low_swap, 3, 1))
+    guarded(4, lambda: swap(own_swap, 4, 1))
+
+    def lower_out():
+        put(total, 0, c, rows(3, c))
+        low_swap.wait_recv()
+        put(total, 0, 1 - c, xr[3])
+        lower.start()
+
+    guarded(3, lower_out)
+    for b in range(3):
+        put(conv_ref, b * 2 * HW, c, rows(b, c))
+    conv_swap.wait_recv()
+    for b in range(3):
+        put(conv_ref, b * 2 * HW, 1 - c, xr[b])
+
+    def own_out():
+        put(out_ref, 0, c, rows(4, c))
+        own_swap.wait_recv()
+        put(out_ref, 0, 1 - c, xr[4])
+        own_swap.wait_send()
+
+    guarded(4, own_out)
+
+    @pl.when(s < NS - 1)
+    def _():
+        lower.wait_recv()
+        out_ref[...] = below[...]
+
+    def lower_end():
+        low_swap.wait_send()
+        lower.wait_send()
+
+    guarded(3, lower_end)
+    conv_swap.wait_send()
+    for b, (r1, r2, _) in enumerate(plans):
+        guarded(b, lambda r1=r1, r2=r2: (r1.drain(), r2.drain()))
 
 
 def remote(src, dst, send, recv, to):
@@ -240,7 +288,8 @@
     ("ct", (SEQS, 2, PB, CH), BF), ("dux", (SEQS, PB, FW), BF), ("dup", (SEQS, PB, FW), BF),
     ("duo", (SEQS, PB, FW), BF), ("extd", (3 * PB, FW), F32), ("dwin", (SEQS, PB, 3 * FW), BF),
     ("dw", (SEQS, 2, PB, 3 * HW), BF), ("dnx", (SEQS, PB, CH), BF),
-    ("hT", (NY, HW, 2 * SEQS * PB), BF), ("cT", (NY, HW, 2 * SEQS * PB), BF),
+    ("hT", (NY, HW, 2 * SEQS * PB), BF), ("cT", (NY, HW, 2 * SEQS * PB), BF), ("tT", (NY, HW, 2 * SEQS * PB), BF),
+    ("gu", (SEQS, 2, PB, HW), BF), ("nx", (SEQS, PB, CH), BF),
 )
 SEMS = (
     ("s_x", (SEQS,)), ("s_w", (2,)), ("s_top", (SEQS,)), ("s_out", (SEQS,)),
@@ -248,6 +297,7 @@
     ("g_s", (SEQS,)), ("g_r", (SEQS,)), ("c_s", (SEQS, NQ)), ("c_r", (SEQS, NQ)),
     ("dp_s", (SEQS,)), ("dp_r", (SEQS,)), ("do_s", (SEQS,)), ("do_r", (SEQS,)),
     ("dw_s", (SEQS, 3)), ("dw_r", (SEQS, 3)), ("hop_s", (SEQS, NQ)), ("hop_r", (SEQS, NQ)),
+    ("n_s", (SEQS,)), ("n_r", (SEQS,)), ("u_s", (SEQS,)), ("u_r", (SEQS,)),
 )
 
 
@@ -257,7 +307,7 @@
     wt = r["wt"]
     xv, wc, wo, hx, ho, gx, exth, uf, su = (r[k] for k in ("xv", "wc", "wo", "hx", "ho", "gx", "exth", "uf", "su"))
     gf, gg, ct, dux, dup, duo, extd = (r[k] for k in ("gf", "gg", "ct", "dux", "dup", "duo", "extd"))
-    dwin, dw, dnx, hT, cT = (r[k] for k in ("dwin", "dw", "dnx", "hT", "cT"))
+    dwin, dw, dnx, hT, cT, tT, gu, nx = (r[k] for k in ("dwin", "dw", "dnx", "hT", "cT", "tT", "gu", "nx"))
     y, z, c = seq_place()
     s = lax.axis_index("section")
     j = seq_at(y, z, c)
@@ -301,6 +351,8 @@
             def _():
                 act(remote(dux.at[b, at], duo.at[b, at], r["do_s"].at[b], r["do_r"].at[b], outer))
 
+    n_near = lambda b: remote(dnx.at[b], nx.at[b], r["n_s"].at[b], r["n_r"].at[b], partner)
+    g_up = lambda b: remote(gg.at[b], gu.at[b], r["u_s"].at[b], r["u_r"].at[b], {"section": lax.min(s + 1, NS - 1)})
     w_near = lambda b, t: remote(dwin.at[b, :, theirs(t)], dw.at[b, 1, :, pl.ds(t * HW, HW)], r["dw_s"].at[b, t], r["dw_r"].at[b, t], partner)
     hop = lambda b, q: remote(dnx.at[b, :, part(q)], ct.at[b, 0, :, part(q)], r["hop_s"].at[b, q], r["hop_r"].at[b, q],
                               {"section": lax.max(s - 1, 0)})
@@ -381,9 +433,26 @@
         for m in range(NY):
             dst[m, :, at] = src[b, :, :, m * HW:(m + 1) * HW].reshape(2 * PB, HW).T
 
+    def turn_lower(b):
+        at = pl.ds(pl.multiple_of(b * 2 * PB, 2 * PB), 2 * PB)
+        n_near(b).wait_recv()
+        for m in range(NY):
+            cols = slice(m * HW, (m + 1) * HW)
+            cT[m, :, at] = jnp.concatenate([dnx[b, :, cols], nx[b, :, cols]], axis=0).T
+
+    def turn_own(b):
+        for q in range(NQ):
+            c_near(b, q).wait_recv()
+        turn(ct, tT, b)
+
+    def send_up(b):
+        g_near(b).wait_recv()
+        g_up(b).start()
+
     @pl.when(s < NS - 1)
     def _():
         loop(SEQS, forward_mid)
+        loop(SEQS, send_up)
         loop(SEQS, lambda b: turn(hx, hT, b))
 
     def front(b):
@@ -398,31 +467,50 @@
         dux[b] = (dg * su[b]).astype(BF)
         d_far(b, lambda one: one.start())
         d_near(b).start()
-        for q in range(NQ):
-            c_near(b, q).start()
 
     def first_front(b):
         forward_mid(b)
         load_top(b).wait()
         front(b)
+        for q in range(NQ):
+            c_near(b, q).start()
 
         @pl.when(b < SEQS - 2)
         def _():
             h_far(b + 2).start()
 
-    @pl.when(s == NS - 1)
-    def _():
-        first_front(0)
+    def any_front(b, more):
+        @pl.when(jnp.logical_and(s < NS - 1, more))
+        def _():
+            front(b)
+
+        @pl.when(jnp.logical_and(s == NS - 1, more))
+        def _():
+            first_front(b)
+
+    def input_grad(b):
+        for q in range(NQ):
+            dh = jnp.dot(dwin[b], wt[:, part(q)], preferred_element_type=F32)
+            dnx[b, :, part(q)] = (ct[b, 0, :, part(q)].astype(F32) + dh * gx[b, :, part(q)]).astype(BF)
+
+            @pl.when(s > 0)
+            def _():
+                hop(b, q).start()
+
+        save(b).start()
+
+        @pl.when(s > 0)
+        def _():
+            n_near(b).start()
 
     def backward(b):
-        @pl.when(s < NS - 1)
-        def _():
-            front(b)
-
-        @pl.when(jnp.logical_and(s == NS - 1, b < SEQS - 1))
-        def _():
-            first_front(b + 1)
-
+        any_front(b + 1, b < SEQS - 1)
+
+        @pl.when(b >= 0)
+        def _():
+            behind(b)
+
+    def behind(b):
         extd[own_at] = dux[b].astype(F32)
         d_near(b).wait_recv()
         extd[near_at] = dup[b].astype(F32)
@@ -431,23 +519,29 @@
         for t in range(3):
             at = pl.ds(pl.multiple_of(PB - (t - 1) * d, 8), PB)
             dwin[b, :, t * FW:(t + 1) * FW] = extd[at].astype(BF)
-        for q in range(NQ):
-            dh = jnp.dot(dwin[b], wt[:, part(q)], preferred_element_type=F32)
-            dnx[b, :, part(q)] = (ct[b, 0, :, part(q)].astype(F32) + dh * gx[b, :, part(q)]).astype(BF)
-
-            @pl.when(s > 0)
-            def _():
-                hop(b, q).start()
-
-        save(b).start()
+        @pl.when(jnp.logical_or(s > 0, b < SEQS - 1))
+        def _():
+            input_grad(b)
+
         for t in range(3):
             w_near(b, t).start()
             dw[b, 0, :, t * HW:(t + 1) * HW] = dwin[b, :, mine(t)]
-        for q in range(NQ):
-            c_near(b, q).wait_recv()
-        turn(ct, cT, b)
-
-    loop(SEQS, backward)
+
+        @pl.when(b > 0)
+        def _():
+            turns(b - 1)
+
+    def turns(b):
+        @pl.when(s > 0)
+        def _():
+            turn_lower(b)
+
+        @pl.when(s == NS - 1)
+        def _():
+            turn_own(b)
+
+    loop(SEQS + 1, lambda i: backward(i - 1))
+    turns(SEQS - 1)
 
     @pl.when(s == NS - 1)
     def _():
@@ -456,18 +550,30 @@
     def gathered(b):
         for t in range(3):
             w_near(b, t).wait_recv()
-        g_near(b).wait_recv()
+
+        @pl.when(s == NS - 1)
+        def _():
+            g_near(b).wait_recv()
+
+        @pl.when(s > 0)
+        def _():
+            g_up(b).wait_recv()
 
     loop(SEQS, gathered)
 
     def fill(b, block):
-        lhs = cT if b == 3 else hT
+        lhs = {3: cT, 4: tT}.get(b, hT)
         for m in range(NY):
-            rhs = gg[...] if b == 3 else dw[:, :, :, b * HW:(b + 1) * HW]
+            rhs = gu[...] if b == 3 else gg[...] if b == 4 else dw[:, :, :, b * HW:(b + 1) * HW]
             got = jnp.dot(lhs[m], rhs.reshape(2 * SEQS * PB, HW), preferred_element_type=F32)
             block[m] = got.reshape(NZ, RB, HW)
 
-    rs_run(fill, scale, conv_ref, out_ref, ring_refs)
+    def beside():
+        @pl.when(s == 0)
+        def _():
+            input_grad(SEQS - 1)
+
+    rs_run(fill, beside, scale, conv_ref, out_ref, ring_refs)
 
     def ended(b):
         save(b).wait()
@@ -478,11 +584,20 @@
         d_far(b, lambda one: one.wait_send())
         for t in range(3):
             w_near(b, t).wait_send()
-        for q in range(NQ):
-            c_near(b, q).wait_send()
-
-            @pl.when(s > 0)
-            def _():
+
+        @pl.when(s == NS - 1)
+        def _():
+            for q in range(NQ):
+                c_near(b, q).wait_send()
+
+        @pl.when(s < NS - 1)
+        def _():
+            g_up(b).wait_send()
+
+        @pl.when(s > 0)
+        def _():
+            n_near(b).wait_send()
+            for q in range(NQ):
                 hop(b, q).wait_send()
 
     loop(SEQS, ended)

time: 123 us -> 115 us (0.935)
  Pallas kernels: 122 us -> 114 us
    pallas_call x1, Pallas kernels: 120 us -> 112 us  [body(): pl.pallas_call(functools.partial(step_kernel, scale), out_shape=(jax.Shap...]
where the time goes in v2:
time: 115 us
  Pallas kernels  114 us (99%)
    pallas_call x1, Pallas kernels, body(): pl.pallas_call(functools.partial(step_kernel, scale), out_shape=(jax.Shap...  112 us

profile of v2, /device:TPU:1, one launch (start us, length us, event | category | flops | bytes accessed | tf_op | source)
XLA Modules:
  0.0 115.0 jit_solution(17452914325034640933)
XLA Ops:
  0.6 112.1 %shard_map.67 = (bf16[1,4,64,1536]{3,2,1,0:T(8,128)(2,1)}, f32[24,2304]{1,0:T(8,128)}, f32[24,768]{1,0:T(8,128)}) custom-call(bf16[1,4,64,1536]{3,2,1,0:T(8,128)(2,1)} %x_hbm.1, bf16[4,64,1536]{2,1,0:T(8,128)(2,1)} %top_hbm.1, bf16[1,1536,2304]{2,1,0:T(8,128)(2,1)} %wc_hbm.1, bf16[1,1536,768]{2,1,0:T(8,128)(2,1)} %wo_hbm.1), custom_call_target="tpu_custom_call" | custom-call | tf_op jit(solution)/shard_map/pallas_call | solution.py:617
  112.7 2.2 %shard_map.68 = (bf16[1,4,64,1536]{3,2,1,0:T(8,128)(2,1)}, f32[1,24,2304]{2,1,0:T(8,128)}, f32[1,24,768]{2,1,0:T(8,128)}) custom-call(bf16[1,4,64,1536]{3,2,1,0:T(8,128)(2,1)} %get-tuple-element.6.a, f32[1,24,2304]{2,1,0:T(8,128)} %bitcast.2, f32[1,24,768]{2,1,0:T(8,128)} %bitcast.3), custom_call_target="tpu_custom_call" | custom-call | tf_op jit(solution)/shard_map/pallas_call | solution.py:634
